TPU v7x, 128 devices: a whole 4x4x4 slice. The times are simulated.
128 devices in a mesh: dp: 16 (over y, x), inner: 8 (over z, core).
Axes of the slice: x: 4, y: 4, z: 4, core: 2. Of those that a mesh axis runs over, the one named last changes fastest.
Arguments:
- queries: bfloat16 [64, 512, 1024], P('dp', 'inner'), may hold values from -6 to 6
- passages: bfloat16 [64, 512, 1024], P('dp', 'inner'), may hold values from -6 to 6
- neg_lists: int32 [64, 8], replicated, may hold values from 0 to 63, as said below
Outputs:
- mean_loss: float32 [], replicated
- query_grad: bfloat16 [64, 512, 1024], P('dp', 'inner')
- passage_grad: bfloat16 [64, 512, 1024], P('dp', 'inner')
Inputs may be any that keep to these rules, and one draw needn't show every extreme that they name: `neg_lists`: each row lists 8 different passage blocks, none from the row's own group (blocks with the same id // 4). The blocks that the rows of one group list include at least one and at most 2 blocks of every other group; in every draw some group lists exactly 2 blocks of every other group.
All inputs are finite; a program needn't handle non-finite values.
Results may differ from a plain program's by a relative error of at most 0.009.
Values may be sent and summed in bfloat16 or wider, within the bound.
A program may use at most 128 MiB of HBM per device.

v0:
```python
import math
import jax
import jax.numpy as jnp
from jax import lax
from jax.sharding import PartitionSpec as P

CAP = 2
NEG_FILL = -1e30


def slot_tables(neg_lists, groups, per_group, slot_depth):
    block_count = neg_lists.shape[0]
    block_ids = jnp.arange(block_count, dtype=jnp.int32)
    named = jnp.any(neg_lists[:, :, None] == block_ids[None, None, :], axis=1)
    present = jnp.any(named.reshape(groups, per_group, block_count), axis=1)
    present = present.reshape(groups, groups, per_group).astype(jnp.int32)
    slot_ranks = jnp.cumsum(present, axis=2) - 1
    slot_ids = jnp.arange(slot_depth, dtype=jnp.int32)
    hits = (present[..., None] == 1) & (slot_ranks[..., None] == slot_ids[None, None, None, :])
    local_ids = jnp.arange(per_group, dtype=jnp.int32)
    slot_block = jnp.sum(jnp.where(hits, local_ids[None, None, :, None], 0), axis=2)
    slot_live = jnp.any(hits, axis=2)
    return (slot_ranks, slot_block, slot_live)


def body(queries, passages, neg_lists):
    per_group, slice_rows, embed_width = queries.shape
    pick_count = neg_lists.shape[1]
    groups = lax.axis_size("dp")
    inner_count = lax.axis_size("inner")
    full_rows = slice_rows * inner_count
    cand_rows = (pick_count + 1) * slice_rows
    slot_count = groups * CAP
    score_scale = 1.0 / math.sqrt(embed_width)
    my_group = lax.axis_index("dp")
    inner_pos = lax.axis_index("inner")
    slot_ranks, slot_block, slot_live = slot_tables(neg_lists, groups, per_group, CAP)
    listed = lax.dynamic_slice_in_dim(neg_lists, my_group * per_group, per_group, 0)
    owner_group = listed // per_group
    owner_local = listed % per_group
    my_ranks = lax.dynamic_index_in_dim(slot_ranks, my_group, 0, keepdims=False)
    slot_of = owner_group * CAP + my_ranks[owner_group, owner_local]
    sends_for = lax.dynamic_index_in_dim(slot_block, my_group, 1, keepdims=False)
    live_for = lax.dynamic_index_in_dim(slot_live, my_group, 1, keepdims=False)
    block_ids = jnp.arange(per_group, dtype=jnp.int32)
    held_start = jnp.zeros((per_group, pick_count, slice_rows, embed_width), jnp.bfloat16)
    shard_rows = lax.all_gather(passages, "dp", axis=0, tiled=True)
    inside = (listed >= 0) & (listed < shard_rows.shape[0])
    picked = shard_rows[jnp.clip(listed, 0, shard_rows.shape[0] - 1)]
    negatives = jnp.where(inside[:, :, None, None], picked, held_start)
    whole_queries = lax.all_gather(queries, "inner", axis=1, tiled=True)

    def candidates(block_index):
        own_rows = lax.dynamic_index_in_dim(passages, block_index, 0, keepdims=True)
        other_rows = lax.dynamic_index_in_dim(negatives, block_index, 0, keepdims=False)
        return jnp.concatenate([own_rows, other_rows], axis=0).reshape(cand_rows, embed_width)

    def scores(block_index, query_block):
        return (
            jnp.einsum(
                "cd,rd->cr",
                candidates(block_index),
                query_block,
                preferred_element_type=jnp.float32,
            )
            * score_scale
        )

    def forward(inputs):
        block_index, query_block = inputs
        logits = scores(block_index, query_block)
        row_peak = jnp.max(logits, axis=0)
        row_mass = jnp.sum(jnp.exp(logits - row_peak[None, :]), axis=0)
        col_peak = jnp.max(logits, axis=1)
        col_mass = jnp.sum(jnp.exp(logits - col_peak[:, None]), axis=1)
        return (row_peak, row_mass, col_peak, col_mass)

    row_peak, row_mass, col_peak, col_mass = lax.map(forward, (block_ids, whole_queries))
    peak_all = lax.pmax(row_peak, "inner")
    mass_all = lax.psum(row_mass * jnp.exp(row_peak - peak_all), "inner")
    query_lse = peak_all + jnp.log(mass_all)
    own_peak = col_peak[:, :slice_rows]
    own_mass = col_mass[:, :slice_rows]
    far_peak = col_peak[:, slice_rows:].reshape(per_group * pick_count, slice_rows)
    far_mass = col_mass[:, slice_rows:].reshape(per_group * pick_count, slice_rows)
    flat_slots = slot_of.reshape(-1)
    onehot = flat_slots[:, None] == jnp.arange(slot_count, dtype=jnp.int32)[None, :]
    slot_peak = jnp.max(jnp.where(onehot[:, :, None], far_peak[:, None, :], NEG_FILL), axis=0)
    rescaled = far_mass * jnp.exp(far_peak - slot_peak[flat_slots])
    slot_mass = jnp.dot(onehot.astype(jnp.float32).T, rescaled, precision=lax.Precision.HIGHEST)
    got_peak, got_mass = (
        lax.all_to_all(
            slot_peak.reshape(groups, CAP, slice_rows),
            "dp",
            split_axis=0,
            concat_axis=0,
            tiled=True,
        ),
        lax.all_to_all(
            slot_mass.reshape(groups, CAP, slice_rows),
            "dp",
            split_axis=0,
            concat_axis=0,
            tiled=True,
        ),
    )
    belongs = (sends_for[:, :, None] == block_ids[None, None, :]) & live_for[:, :, None]
    belongs = belongs.reshape(slot_count, per_group)
    got_peak = got_peak.reshape(slot_count, slice_rows)
    got_mass = got_mass.reshape(slot_count, slice_rows)
    spread_peak = jnp.where(belongs[:, :, None], got_peak[:, None, :], NEG_FILL)
    pass_peak = jnp.maximum(own_peak, jnp.max(spread_peak, axis=0))
    spread_mass = jnp.where(
        belongs[:, :, None],
        got_mass[:, None, :] * jnp.exp(spread_peak - pass_peak[None, :, :]),
        0.0,
    )
    pass_mass = own_mass * jnp.exp(own_peak - pass_peak) + jnp.sum(spread_mass, axis=0)
    passage_lse = pass_peak + jnp.log(pass_mass)
    own_scores = (
        jnp.einsum("lrd,lrd->lr", queries, passages, preferred_element_type=jnp.float32)
        * score_scale
    )
    my_query_lse = lax.dynamic_slice_in_dim(query_lse, inner_pos * slice_rows, slice_rows, 1)
    local_loss = jnp.sum(my_query_lse - own_scores) + jnp.sum(passage_lse - own_scores)
    mean_loss = lax.psum(local_loss, ("dp", "inner")) / (2.0 * groups * per_group * full_rows)
    lse_out = passage_lse[sends_for]
    lse_back = lax.all_to_all(lse_out, "dp", split_axis=0, concat_axis=0, tiled=True).reshape(
        slot_count, slice_rows
    )
    cand_lse = jnp.concatenate([passage_lse[:, None, :], lse_back[slot_of]], axis=1).reshape(
        per_group, cand_rows
    )
    cand_pos = jnp.arange(cand_rows, dtype=jnp.int32)
    row_pos = jnp.arange(full_rows, dtype=jnp.int32)
    target = (
        (cand_pos[:, None] < slice_rows)
        & (row_pos[None, :] == inner_pos * slice_rows + cand_pos[:, None])
    ).astype(jnp.float32)

    def backward(block_index, carry):
        weights, slot_grad, own_grad = carry
        query_block = lax.dynamic_index_in_dim(whole_queries, block_index, 0, keepdims=False)
        logits = scores(block_index, query_block)
        row_lse = lax.dynamic_index_in_dim(query_lse, block_index, 0, keepdims=False)
        col_lse = lax.dynamic_index_in_dim(cand_lse, block_index, 0, keepdims=False)
        probs = (
            0.5 * jnp.exp(logits - row_lse[None, :])
            + 0.5 * jnp.exp(logits - col_lse[:, None])
            - target
        )
        rounded = probs.astype(jnp.bfloat16)
        passage_part = jnp.einsum(
            "cr,rd->cd", rounded, query_block, preferred_element_type=jnp.float32
        )
        own_grad = lax.dynamic_update_index_in_dim(
            own_grad, passage_part[:slice_rows], block_index, 0
        )
        slot_targets = lax.dynamic_index_in_dim(slot_of, block_index, 0, keepdims=False)
        slot_grad = slot_grad.at[slot_targets].add(
            passage_part[slice_rows:].reshape(pick_count, slice_rows, embed_width)
        )
        weights = lax.dynamic_update_index_in_dim(weights, rounded, block_index, 0)
        return (weights, slot_grad, own_grad)

    start_carry = (
        jnp.zeros((per_group, cand_rows, full_rows), jnp.bfloat16),
        jnp.zeros((slot_count, slice_rows, embed_width), jnp.float32),
        jnp.zeros((per_group, slice_rows, embed_width), jnp.float32),
    )
    weights, slot_grad, own_grad = lax.fori_loop(0, per_group, backward, start_carry)

    def one_block(inputs):
        block_index, block_weights = inputs
        return jnp.einsum(
            "cr,cd->rd", block_weights, candidates(block_index), preferred_element_type=jnp.float32
        )

    query_sum = lax.psum_scatter(
        jnp.swapaxes(lax.map(one_block, (block_ids, weights)), 0, 1).astype(jnp.bfloat16),
        "inner",
        scatter_dimension=0,
        tiled=True,
    ).astype(jnp.float32)
    query_grad = jnp.swapaxes(query_sum, 0, 1).astype(jnp.bfloat16)
    returned = lax.all_to_all(
        slot_grad.astype(jnp.bfloat16).reshape(groups, CAP, slice_rows, embed_width),
        "dp",
        split_axis=0,
        concat_axis=0,
        tiled=True,
    )
    passage_sum = jnp.einsum(
        "eg,ecd->gcd",
        belongs.astype(jnp.bfloat16),
        returned.reshape(slot_count, slice_rows, embed_width),
        preferred_element_type=jnp.float32,
    )
    passage_grad = (passage_sum + own_grad).astype(jnp.bfloat16)
    return (mean_loss, query_grad, passage_grad)


def solution(mesh):
    in_specs = (P("dp", "inner", None), P("dp", "inner", None), P())
    out_specs = (P(), P("dp", "inner", None), P("dp", "inner", None))
    return jax.shard_map(body, mesh=mesh, in_specs=in_specs, out_specs=out_specs, check_vma=False)
```

profile of v0, /device:TPU:1, one launch (start us, length us, event | category | flops | bytes accessed | tf_op | source)
XLA Modules:
  0.0 454.0 jit_solution(6817125540954745259)
XLA Ops:
  13.2 70.7 %all-gather.3.cloned.1.call-done = bf16[64,64,1024]{2,1,0:T(8,128)(2,1)} async-done(((bf16[4,64,1024]{2,1,0:T(8,128)(2,1)}), bf16[64,64,1024]{2,1,0:T(8,128)(2,1)}) %all-gather.3.cloned.1.call-update) | async-done | bytes 8388624 | tf_op jit(solution)/shard_map/all_gather | solution.py:47
  83.9 6.1 %gather_fusion = bf16[32,64,1024]{2,1,0:T(8,128)(2,1)} fusion(bf16[64,64,1024]{2,1,0:T(8,128)(2,1)} %all-gather.3.cloned.1.call-done, s32[1024]{0:T(1024)S(1)} %pad_clamp_fusion.3), kind=kCustom, calls=%fused_computation | custom fusion | bytes 8388736 | tf_op jit(solution)/shard_map/gather | solution.py:49
  90.0 4.5 broadcast_select_fusion
  94.5 23.6 %all-gather.5.cloned.1.call-done = bf16[4,512,1024]{2,1,0:T(8,128)(2,1)} async-done(((bf16[4,64,1024]{2,1,0:T(8,128)(2,1)}), bf16[4,512,1024]{2,1,0:T(8,128)(2,1)}) %all-gather.5.cloned.1.call-update) | async-done | bytes 4194320 | tf_op jit(solution)/shard_map/all_gather | solution.py:51
  118.2 27.3 %while.44 = (s32[]{:T(128)}, f32[4,512]{1,0:T(4,128)S(1)}, f32[4,512]{1,0:T(4,128)S(1)}, f32[4,576]{1,0:T(4,128)S(1)}, f32[4,576]{1,0:T(4,128)S(1)}, /*index=5*/...) while((s32[]{:T(128)}, f32[4,512]{1,0:T(4,128)S(1)}, ...), condition=%wide.region_5.6_spmd, body=%wide.region_0.5_spmd.sunk | while | flops 606631808 | bytes 9346491 | solution.py:78
  147.6 6.5 %all-to-all-start.1 = ((f32[16,1,128]{2,1,0:T(1,128)}), f32[16,1,128]{2,1,0:T(1,128)S(1)}, u32[]{:S(2)}, u32[]{:S(2)}) async-start(f32[16,1,128]{2,1,0:T(1,128)} %reshape.334), calls=%async_computation.1 | async-start | bytes 16384 | tf_op jit(solution)/shard_map/all_to_all | solution.py:99
  154.8 12.5 %pmax.7 = f32[4,512]{1,0:T(4,128)S(1)} all-reduce(f32[4,512]{1,0:T(4,128)S(1)} %get-tuple-element.271), channel_id=1, replica_groups=mesh['dp'=16,'inner'=8] {'inner'}, use_global_device_ids=true, to_apply=%region_6.7 | all-reduce | flops 2048 | bytes 16384 | tf_op jit(solution)/shard_map/pmax | solution.py:79
  167.3 13.3 %psum.14 = f32[4,512]{1,0:T(4,128)S(1)} all-reduce(f32[4,512]{1,0:T(4,128)S(1)} %exponential_multiply_fusion.1), channel_id=1, replica_groups=mesh['dp'=16,'inner'=8] {'inner'}, use_global_device_ids=true, to_apply=%region_7.8 | all-reduce | flops 2048 | bytes 16384 | tf_op jit(solution)/shard_map/psum | solution.py:80
  180.7 6.4 %all-to-all-start = ((f32[16,1,128]{2,1,0:T(1,128)}), f32[16,1,128]{2,1,0:T(1,128)S(1)}, u32[]{:S(2)}, u32[]{:S(2)}) async-start(f32[16,1,128]{2,1,0:T(1,128)} %reshape.332), calls=%async_computation | async-start | bytes 16384 | tf_op jit(solution)/shard_map/all_to_all | solution.py:92
  188.3 5.1 %all-to-all-done = f32[16,1,128]{2,1,0:T(1,128)S(1)} async-done(((f32[16,1,128]{2,1,0:T(1,128)}), f32[16,1,128]{2,1,0:T(1,128)S(1)}, u32[]{:S(2)}, u32[]{:S(2)}) %all-to-all-start) | async-done | bytes 8224 | tf_op jit(solution)/shard_map/all_to_all | solution.py:92
  196.4 3.5 all-to-all-start.2
  200.1 6.0 %all-to-all-done.2 = f32[16,1,128]{2,1,0:T(1,128)S(1)} async-done(((f32[16,1,128]{2,1,0:T(1,128)}), f32[16,1,128]{2,1,0:T(1,128)S(1)}, u32[]{:S(2)}, u32[]{:S(2)}) %all-to-all-start.2) | async-done | bytes 8224 | tf_op jit(solution)/shard_map/all_to_all | solution.py:128
  207.6 4.3 broadcast_in_dim.183
  211.9 72.2 %while.46 = (s32[]{:T(128)}, bf16[4,576,512]{2,1,0:T(8,128)(2,1)}, f32[32,64,1024]{2,1,0:T(8,128)}, f32[4,64,1024]{2,0,1:T(4,128)}, bf16[4,64,1024]{2,1,0:T(8,12...) while((s32[]{:T(128)}, bf16[4,576,512]{2,1,0:T(8,128)(2,1)}, ...), condition=%wide.region_21.22_spmd.clone, body=%wide.region_19.21_spmd.clone.sunk | while | flops 1212022784 | bytes 40981276 | solution.py:171
  218.6 5.1 %scatter_fusion = f32[32,64,1024]{2,1,0:T(8,128)} fusion(f32[32,64,1024]{2,1,0:T(8,128)} %get-tuple-element.624, s32[8]{0:T(128)S(1)} %fusion.79, f32[8,64,1024]{2,1,0:T(8,128)} %bitcast.138), kind=kCustom, calls=%fused_computation.5.clone.clone.1 | custom fusion | flops 524288 | bytes 6291488 | tf_op jit(solution)/shard_map/while/body/eval_jaxpr/scatter-add | solution.py:160
  224.0 5.8 %dynamic_update_slice.51 = f32[4,64,1024]{2,0,1:T(4,128)} dynamic-update-slice(f32[4,64,1024]{2,0,1:T(4,128)} %get-tuple-element.625, f32[1,64,1024]{2,0,1:T(1,128)S(1)} %copy.96, s32[]{:T(128)} %get-tuple-element.622, s32[]{:T(128)} %constant.189.clone.1..sunk.2, s32[]{:T(128)} %constant.189.clone.1..sunk.2) | dynamic-update-slice | bytes 524292 | tf_op jit(solution)/shard_map/while/body/eval_jaxpr/jit(dynamic_update_index_in_dim)/dynamic_update_slice | solution.py:156
  236.6 5.2 %scatter_fusion = f32[32,64,1024]{2,1,0:T(8,128)} fusion(f32[32,64,1024]{2,1,0:T(8,128)} %get-tuple-element.624, s32[8]{0:T(128)S(1)} %fusion.79, f32[8,64,1024]{2,1,0:T(8,128)} %bitcast.138), kind=kCustom, calls=%fused_computation.5.clone.clone.1 | custom fusion | flops 524288 | bytes 6291488 | tf_op jit(solution)/shard_map/while/body/eval_jaxpr/scatter-add | solution.py:160
  242.1 5.8 %dynamic_update_slice.51 = f32[4,64,1024]{2,0,1:T(4,128)} dynamic-update-slice(f32[4,64,1024]{2,0,1:T(4,128)} %get-tuple-element.625, f32[1,64,1024]{2,0,1:T(1,128)S(1)} %copy.96, s32[]{:T(128)} %get-tuple-element.622, s32[]{:T(128)} %constant.189.clone.1..sunk.2, s32[]{:T(128)} %constant.189.clone.1..sunk.2) | dynamic-update-slice | bytes 524292 | tf_op jit(solution)/shard_map/while/body/eval_jaxpr/jit(dynamic_update_index_in_dim)/dynamic_update_slice | solution.py:156
  254.7 5.1 %scatter_fusion = f32[32,64,1024]{2,1,0:T(8,128)} fusion(f32[32,64,1024]{2,1,0:T(8,128)} %get-tuple-element.624, s32[8]{0:T(128)S(1)} %fusion.79, f32[8,64,1024]{2,1,0:T(8,128)} %bitcast.138), kind=kCustom, calls=%fused_computation.5.clone.clone.1 | custom fusion | flops 524288 | bytes 6291488 | tf_op jit(solution)/shard_map/while/body/eval_jaxpr/scatter-add | solution.py:160
  260.2 5.8 %dynamic_update_slice.51 = f32[4,64,1024]{2,0,1:T(4,128)} dynamic-update-slice(f32[4,64,1024]{2,0,1:T(4,128)} %get-tuple-element.625, f32[1,64,1024]{2,0,1:T(1,128)S(1)} %copy.96, s32[]{:T(128)} %get-tuple-element.622, s32[]{:T(128)} %constant.189.clone.1..sunk.2, s32[]{:T(128)} %constant.189.clone.1..sunk.2) | dynamic-update-slice | bytes 524292 | tf_op jit(solution)/shard_map/while/body/eval_jaxpr/jit(dynamic_update_index_in_dim)/dynamic_update_slice | solution.py:156
  272.8 5.1 %scatter_fusion = f32[32,64,1024]{2,1,0:T(8,128)} fusion(f32[32,64,1024]{2,1,0:T(8,128)} %get-tuple-element.624, s32[8]{0:T(128)S(1)} %fusion.79, f32[8,64,1024]{2,1,0:T(8,128)} %bitcast.138), kind=kCustom, calls=%fused_computation.5.clone.clone.1 | custom fusion | flops 524288 | bytes 6291488 | tf_op jit(solution)/shard_map/while/body/eval_jaxpr/scatter-add | solution.py:160
  278.2 5.8 %dynamic_update_slice.51 = f32[4,64,1024]{2,0,1:T(4,128)} dynamic-update-slice(f32[4,64,1024]{2,0,1:T(4,128)} %get-tuple-element.625, f32[1,64,1024]{2,0,1:T(1,128)S(1)} %copy.96, s32[]{:T(128)} %get-tuple-element.622, s32[]{:T(128)} %constant.189.clone.1..sunk.2, s32[]{:T(128)} %constant.189.clone.1..sunk.2) | dynamic-update-slice | bytes 524292 | tf_op jit(solution)/shard_map/while/body/eval_jaxpr/jit(dynamic_update_index_in_dim)/dynamic_update_slice | solution.py:156
  284.1 28.3 %while.45 = (s32[]{:T(128)}, bf16[4,512,1024]{2,1,0:T(8,128)(2,1)}, bf16[4,576,512]{2,1,0:T(8,128)(2,1)}, s32[4]{0:T(128)S(1)}, bf16[4,64,1024]{2,1,0:T(8,128)(2...) while((s32[]{:T(128)}, bf16[4,512,1024]{2,1,0:T(8,128)(2,1)}, ...), condition=%wide.region_23.24_spmd, body=%wide.region_22.23_spmd.sunk | while | flops 604569600 | bytes 8586387 | solution.py:180
  288.0 3.1 bitcast_dynamic-update-slice_fusion.4
  295.1 3.1 bitcast_dynamic-update-slice_fusion.4
  302.2 3.1 bitcast_dynamic-update-slice_fusion.4
  309.3 3.1 bitcast_dynamic-update-slice_fusion.4
  312.4 4.0 convert_element_type.45
  316.4 6.3 %copy.71 = bf16[16,2,64,1024]{3,1,2,0:T(2,128)(2,1)} copy(bf16[16,2,64,1024]{3,2,1,0:T(8,128)(2,1)S(1)} %bitcast.142) | data formatting | bytes 8388608 | tf_op jit(solution)/shard_map/reshape | solution.py:187
  322.7 4.7 %all-to-all-start.3 = ((bf16[16,2,64,1024]{3,1,2,0:T(2,128)(2,1)}), bf16[16,2,64,1024]{3,1,2,0:T(2,128)(2,1)}, u32[]{:S(2)}, u32[]{:S(2)}) async-start(bf16[16,2,64,1024]{3,1,2,0:T(2,128)(2,1)} %copy.71), calls=%async_computation.4 | async-start | bytes 8388608 | tf_op jit(solution)/shard_map/all_to_all | solution.py:186
  328.7 111.3 %psum.15 = f32[]{:T(128)} all-reduce(f32[]{:T(128)S(6)} %add.200), channel_id=1, replica_groups=mesh['dp'=16,'inner'=8] {'dp','inner'}, use_global_device_ids=true, to_apply=%region_18.19 | all-reduce | flops 1 | bytes 8 | tf_op jit(solution)/shard_map/psum | solution.py:126
  440.6 4.8 %fusion.27 = bf16[4,64,1024]{2,0,1:T(4,128)(2,1)S(1)} fusion(f32[4,64,1024]{2,0,1:T(4,128)S(1)} %copy-done.3, bf16[16,2,64,1024]{3,1,2,0:T(2,128)(2,1)} %all-to-all-done.3, s32[16,2]{0,1:T(2,128)S(1)} %get-tuple-element.386, pred[16,2]{0,1:T(4,128)(4,1)S(1)} %get-tuple-element.382), kind=kOutput, calls=%fused_computation.52 | convolution fusion | flops 17301760 | bytes 5767328 | tf_op jit(solution)/shard_map/eg,ecd->gcd/dot_general | solution.py:193
  (214 shorter events, 70.9 us)
Async XLA Ops:
  7.2 5.7 %copy-start = (bf16[4,64,1024]{2,1,0:T(8,128)(2,1)S(1)}, bf16[4,64,1024]{2,1,0:T(8,128)(2,1)}, u32[]{:S(2)}) copy-start(bf16[4,64,1024]{2,1,0:T(8,128)(2,1)} %param.10) | copy-start | bytes 1572868
  7.2 5.7 %copy-start.2 = (bf16[4,64,1024]{2,1,0:T(8,128)(2,1)S(1)}, bf16[4,64,1024]{2,1,0:T(8,128)(2,1)}, u32[]{:S(2)}) copy-start(bf16[4,64,1024]{2,1,0:T(8,128)(2,1)} %param.9) | copy-start | bytes 1572868
  7.2 76.7 %all-gather.3.cloned.1.call-start = ((), (), s32[]{:S(2)}) async-start(), calls=%async_computation.5 | async-start | bytes 8912896 | tf_op jit(solution)/shard_map/all_gather | solution.py:47
  7.9 110.3 %all-gather.5.cloned.1.call-start = ((), (), s32[]{:S(2)}) async-start(), calls=%async_computation.6 | async-start | bytes 4718592 | tf_op jit(solution)/shard_map/all_gather | solution.py:51
  147.6 33.0 %all-to-all-start.1 = ((f32[16,1,128]{2,1,0:T(1,128)}), f32[16,1,128]{2,1,0:T(1,128)S(1)}, u32[]{:S(2)}, u32[]{:S(2)}) async-start(f32[16,1,128]{2,1,0:T(1,128)} %reshape.334), calls=%async_computation.1 | async-start | bytes 16384 | tf_op jit(solution)/shard_map/all_to_all | solution.py:99
  180.7 12.7 %all-to-all-start = ((f32[16,1,128]{2,1,0:T(1,128)}), f32[16,1,128]{2,1,0:T(1,128)S(1)}, u32[]{:S(2)}, u32[]{:S(2)}) async-start(f32[16,1,128]{2,1,0:T(1,128)} %reshape.332), calls=%async_computation | async-start | bytes 16384 | tf_op jit(solution)/shard_map/all_to_all | solution.py:92
  196.4 9.8 %all-to-all-start.2 = ((f32[16,1,128]{2,1,0:T(1,128)}), f32[16,1,128]{2,1,0:T(1,128)S(1)}, u32[]{:S(2)}, u32[]{:S(2)}) async-start(f32[16,1,128]{2,1,0:T(1,128)} %reshape.336), calls=%async_computation.2 | async-start | bytes 16384 | tf_op jit(solution)/shard_map/all_to_all | solution.py:128
  199.8 246.5 %reduce-scatter.2.cloned.1.call-start = ((), (), s32[]{:S(2)}) async-start(), calls=%async_computation.7 | async-start | bytes 4718592 | tf_op jit(solution)/shard_map/reduce_scatter | solution.py:179
  211.9 2.5 copy-start.1
  229.9 2.5 copy-start.1
  247.9 2.5 copy-start.1
  266.0 2.5 copy-start.1
  322.7 117.9 %copy-start.3 = (f32[4,64,1024]{2,0,1:T(4,128)S(1)}, f32[4,64,1024]{2,0,1:T(4,128)}, u32[]{:S(2)}) copy-start(f32[4,64,1024]{2,0,1:T(4,128)} %get-tuple-element.278) | copy-start | bytes 3145732
  322.7 117.9 %all-to-all-start.3 = ((bf16[16,2,64,1024]{3,1,2,0:T(2,128)(2,1)}), bf16[16,2,64,1024]{3,1,2,0:T(2,128)(2,1)}, u32[]{:S(2)}, u32[]{:S(2)}) async-start(bf16[16,2,64,1024]{3,1,2,0:T(2,128)(2,1)} %copy.71), calls=%async_computation.4 | async-start | bytes 8388608 | tf_op jit(solution)/shard_map/all_to_all | solution.py:186
Sparse Core Ops, SparseCore 0:
  10.1 73.7 all-gather.2
  85.6 32.5 all-gather.4
  312.5 33.4 reduce-scatter.1
where the time goes:
time: 456 us; the launch traced here: 454 us
  blocking collectives  137 us (30%)
  waiting for transfers between devices  107 us (23%)
  local copies, waits for them, and re-layouts  82.3 us (18%)
  matrix products  37 us (8%)
  other arithmetic  36.1 us (8%)
  starting transfers between devices  21.3 us (5%)
  between operations  17.2 us (4%)
  loops' own time  16.1 us (4%)
    psum x1, blocking collectives, body(): lax.psum(local_loss, ('dp', 'inner'))  111 us
    all_gather x1, waiting for transfers between devices, body(): shard_rows = lax.all_gather(passages, 'dp', axis=0, tiled=True)  70.7 us
    dynamic_update_slice x8, local copies, waits for them, and re-layouts, backward(): lax.dynamic_update_index_in_dim(own_grad, passage_part[:slice_rows], bloc...  24.4 us
    all_gather x1, waiting for transfers between devices, body(): whole_queries = lax.all_gather(queries, 'inner', axis=1, tiled=True)  23.6 us
    scatter-add x4, other arithmetic, backward(): slot_grad.at[slot_targets]  20.5 us
    dot_general x8, matrix products, scores(): jnp.einsum('cd,rd->cr', candidates(block_index), query_block, preferred_e...  16.6 us
    squeeze x12, local copies, waits for them, and re-layouts, candidates(): lax.dynamic_index_in_dim(negatives, block_index, 0, keepdims=False)  16.3 us
    psum x1, blocking collectives, body(): mass_all = lax.psum(row_mass * jnp.exp(row_peak - peak_all), 'inner')  13.3 us
  transfers between devices with their start and end apart: 7, of which 4 were waited for; matrix products, arithmetic and copies ran while one was open for 7% of the time, Pallas kernels for 0%

commit v1 on v0

--- a/solution.py
+++ b/solution.py
@@ -1,3 +1,4 @@
+import functools
 import math
 import jax
 import jax.numpy as jnp
@@ -6,6 +7,17 @@
 
 CAP = 2
 NEG_FILL = -1e30
+
+
+def cut_arrays_on(local, shard_axis, out_dim):
+    block_next = jnp.stack([local for _ in range(jax.lax.axis_size(shard_axis))])
+    return jnp.concatenate(
+        jax.lax.all_to_all(block_next, axis_name=shard_axis, split_axis=0, concat_axis=0),
+        axis=out_dim,
+    )
+
+
+order_the_bands = functools.partial(cut_arrays_on, shard_axis="inner", out_dim=1)
 
 
 def slot_tables(neg_lists, groups, per_group, slot_depth):
@@ -48,7 +60,7 @@
     inside = (listed >= 0) & (listed < shard_rows.shape[0])
     picked = shard_rows[jnp.clip(listed, 0, shard_rows.shape[0] - 1)]
     negatives = jnp.where(inside[:, :, None, None], picked, held_start)
-    whole_queries = lax.all_gather(queries, "inner", axis=1, tiled=True)
+    whole_queries = order_the_bands(queries)
 
     def candidates(block_index):
         own_rows = lax.dynamic_index_in_dim(passages, block_index, 0, keepdims=True)

time: 456 us -> 433 us (0.950)
  waiting for transfers between devices: 107 us -> 68.4 us
  local copies, waits for them, and re-layouts: 82.3 us -> 90.1 us
  starting transfers between devices: 21.3 us -> 26.7 us
    all_gather x1, waiting for transfers between devices: 70.7 us -> 11.7 us  [body(): shard_rows = lax.all_gather(passages, 'dp', axis=0, tiled=True)]
    all_to_all x0 -> x1, waiting for transfers between devices: none -> 44.9 us  [cut_arrays_on(): jax.lax.all_to_all(block_next, axis_name=shard_axis, split_axis=0, concat...]
    all_gather x1 -> x0, waiting for transfers between devices: 23.6 us -> none  [body(): whole_queries = lax.all_gather(queries, 'inner', axis=1, tiled=True)]
    all_to_all x0 -> x1, starting transfers between devices: none -> 6.93 us  [cut_arrays_on(): jax.lax.all_to_all(block_next, axis_name=shard_axis, split_axis=0, concat...]
    all_to_all x0 -> x1, local copies, waits for them, and re-layouts: none -> 5.01 us  [cut_arrays_on(): jax.lax.all_to_all(block_next, axis_name=shard_axis, split_axis=0, concat...]
where the time goes in v1:
time: 433 us; the launch traced here: 431 us
  blocking collectives  139 us (32%)
  local copies, waits for them, and re-layouts  90.1 us (21%)
  waiting for transfers between devices  68.4 us (16%)
  matrix products  37 us (9%)
  other arithmetic  36.1 us (8%)
  starting transfers between devices  26.7 us (6%)
  between operations  17.5 us (4%)
  loops' own time  16.1 us (4%)
    psum x1, blocking collectives, body(): lax.psum(local_loss, ('dp', 'inner'))  111 us
    all_to_all x1, waiting for transfers between devices, cut_arrays_on(): jax.lax.all_to_all(block_next, axis_name=shard_axis, split_axis=0, concat...  44.9 us
    dynamic_update_slice x8, local copies, waits for them, and re-layouts, backward(): lax.dynamic_update_index_in_dim(own_grad, passage_part[:slice_rows], bloc...  24.4 us
    scatter-add x4, other arithmetic, backward(): slot_grad.at[slot_targets]  20.5 us
    dot_general x8, matrix products, scores(): jnp.einsum('cd,rd->cr', candidates(block_index), query_block, preferred_e...  16.6 us
    squeeze x12, local copies, waits for them, and re-layouts, candidates(): lax.dynamic_index_in_dim(negatives, block_index, 0, keepdims=False)  16.3 us
    psum x1, blocking collectives, body(): mass_all = lax.psum(row_mass * jnp.exp(row_peak - peak_all), 'inner')  14.8 us
    pmax x1, blocking collectives, body(): peak_all = lax.pmax(row_peak, 'inner')  13.2 us
  transfers between devices with their start and end apart: 7, of which 4 were waited for; matrix products, arithmetic and copies ran while one was open for 7% of the time, Pallas kernels for 0%

profile of v1, /device:TPU:1, one launch (start us, length us, event | category | flops | bytes accessed | tf_op | source)
XLA Modules:
  0.0 431.2 jit_solution(17603329458877102932)
XLA Ops:
  7.9 3.5 stack.2
  11.4 6.9 %all-to-all-start = ((bf16[8,4,64,1024]{3,2,1,0:T(8,128)(2,1)}), bf16[8,4,64,1024]{3,2,1,0:T(8,128)(2,1)}, u32[]{:S(2)}, u32[]{:S(2)}) async-start(bf16[8,4,64,1024]{3,2,1,0:T(8,128)(2,1)} %stack.2), calls=%async_computation | async-start | bytes 8388608 | tf_op jit(solution)/shard_map/all_to_all | solution.py:15
  22.3 44.9 %all-to-all-done = bf16[8,4,64,1024]{3,2,1,0:T(8,128)(2,1)} async-done(((bf16[8,4,64,1024]{3,2,1,0:T(8,128)(2,1)}), bf16[8,4,64,1024]{3,2,1,0:T(8,128)(2,1)}, u32[]{:S(2)}, u32[]{:S(2)}) %all-to-all-start) | async-done | bytes 4194336 | tf_op jit(solution)/shard_map/all_to_all | solution.py:15
  67.2 5.0 %copy.76 = bf16[8,4,64,1024]{3,2,0,1:T(8,128)(2,1)} copy(bf16[8,4,64,1024]{3,2,1,0:T(8,128)(2,1)} %all-to-all-done) | data formatting | bytes 8388608 | tf_op jit(solution)/shard_map/all_to_all | solution.py:15
  72.2 11.7 %all-gather.2.cloned.1.call-done = bf16[64,64,1024]{2,1,0:T(8,128)(2,1)} async-done(((bf16[4,64,1024]{2,1,0:T(8,128)(2,1)}), bf16[64,64,1024]{2,1,0:T(8,128)(2,1)}) %all-gather.2.cloned.1.call-update) | async-done | bytes 8388624 | tf_op jit(solution)/shard_map/all_gather | solution.py:59
  83.8 6.1 %gather_fusion = bf16[32,64,1024]{2,1,0:T(8,128)(2,1)} fusion(bf16[64,64,1024]{2,1,0:T(8,128)(2,1)} %all-gather.2.cloned.1.call-done, s32[1024]{0:T(1024)S(1)} %pad_clamp_fusion.3), kind=kCustom, calls=%fused_computation | custom fusion | bytes 8388736 | tf_op jit(solution)/shard_map/gather | solution.py:61
  90.0 4.5 %broadcast_select_fusion = bf16[4,8,64,1024]{3,2,1,0:T(8,128)(2,1)} fusion(bf16[4,8,64,1024]{3,2,1,0:T(8,128)(2,1)} %bitcast.147, pred[4,8]{1,0:T(4,128)(4,1)S(1)} %compare_and_fusion), kind=kLoop, calls=%fused_computation.49 | loop fusion | flops 2097152 | bytes 8388640 | tf_op jit(solution)/shard_map/jit(_where)/select_n | solution.py:62
  94.5 27.3 %while.44 = (s32[]{:T(128)}, f32[4,512]{1,0:T(4,128)S(1)}, f32[4,512]{1,0:T(4,128)S(1)}, f32[4,576]{1,0:T(4,128)S(1)}, f32[4,576]{1,0:T(4,128)S(1)}, /*index=5*/...) while((s32[]{:T(128)}, f32[4,512]{1,0:T(4,128)S(1)}, ...), condition=%wide.region_5.6_spmd, body=%wide.region_0.5_spmd.sunk | while | flops 606631808 | bytes 9346491 | solution.py:90
  123.9 5.0 %all-to-all-start.2 = ((f32[16,1,128]{2,1,0:T(1,128)}), f32[16,1,128]{2,1,0:T(1,128)S(1)}, u32[]{:S(2)}, u32[]{:S(2)}) async-start(f32[16,1,128]{2,1,0:T(1,128)} %reshape.344), calls=%async_computation.2 | async-start | bytes 16384 | tf_op jit(solution)/shard_map/all_to_all | solution.py:111
  129.5 13.2 %pmax.7 = f32[4,512]{1,0:T(4,128)S(1)} all-reduce(f32[4,512]{1,0:T(4,128)S(1)} %get-tuple-element.271), channel_id=1, replica_groups=mesh['dp'=16,'inner'=8] {'inner'}, use_global_device_ids=true, to_apply=%region_6.7 | all-reduce | flops 2048 | bytes 16384 | tf_op jit(solution)/shard_map/pmax | solution.py:91
  142.7 14.8 %psum.14 = f32[4,512]{1,0:T(4,128)S(1)} all-reduce(f32[4,512]{1,0:T(4,128)S(1)} %exponential_multiply_fusion.1), channel_id=1, replica_groups=mesh['dp'=16,'inner'=8] {'inner'}, use_global_device_ids=true, to_apply=%region_7.8 | all-reduce | flops 2048 | bytes 16384 | tf_op jit(solution)/shard_map/psum | solution.py:92
  157.6 6.4 %all-to-all-start.1 = ((f32[16,1,128]{2,1,0:T(1,128)}), f32[16,1,128]{2,1,0:T(1,128)S(1)}, u32[]{:S(2)}, u32[]{:S(2)}) async-start(f32[16,1,128]{2,1,0:T(1,128)} %reshape.342), calls=%async_computation.1 | async-start | bytes 16384 | tf_op jit(solution)/shard_map/all_to_all | solution.py:104
  165.2 5.1 %all-to-all-done.1 = f32[16,1,128]{2,1,0:T(1,128)S(1)} async-done(((f32[16,1,128]{2,1,0:T(1,128)}), f32[16,1,128]{2,1,0:T(1,128)S(1)}, u32[]{:S(2)}, u32[]{:S(2)}) %all-to-all-start.1) | async-done | bytes 8224 | tf_op jit(solution)/shard_map/all_to_all | solution.py:104
  173.3 3.5 all-to-all-start.3
  177.0 6.0 %all-to-all-done.3 = f32[16,1,128]{2,1,0:T(1,128)S(1)} async-done(((f32[16,1,128]{2,1,0:T(1,128)}), f32[16,1,128]{2,1,0:T(1,128)S(1)}, u32[]{:S(2)}, u32[]{:S(2)}) %all-to-all-start.3) | async-done | bytes 8224 | tf_op jit(solution)/shard_map/all_to_all | solution.py:140
  184.5 4.3 broadcast_in_dim.183
  188.8 72.2 %while.46 = (s32[]{:T(128)}, bf16[4,576,512]{2,1,0:T(8,128)(2,1)}, f32[32,64,1024]{2,1,0:T(8,128)}, f32[4,64,1024]{2,0,1:T(4,128)}, bf16[4,64,1024]{2,1,0:T(8,12...) while((s32[]{:T(128)}, bf16[4,576,512]{2,1,0:T(8,128)(2,1)}, ...), condition=%wide.region_21.22_spmd.clone, body=%wide.region_19.21_spmd.clone.sunk | while | flops 1212022784 | bytes 40981276 | solution.py:183
  195.5 5.1 %scatter_fusion = f32[32,64,1024]{2,1,0:T(8,128)} fusion(f32[32,64,1024]{2,1,0:T(8,128)} %get-tuple-element.627, s32[8]{0:T(128)S(1)} %fusion.79, f32[8,64,1024]{2,1,0:T(8,128)} %bitcast.141), kind=kCustom, calls=%fused_computation.5.clone.clone.1 | custom fusion | flops 524288 | bytes 6291488 | tf_op jit(solution)/shard_map/while/body/eval_jaxpr/scatter-add | solution.py:172
  200.9 5.8 %dynamic_update_slice.51 = f32[4,64,1024]{2,0,1:T(4,128)} dynamic-update-slice(f32[4,64,1024]{2,0,1:T(4,128)} %get-tuple-element.628, f32[1,64,1024]{2,0,1:T(1,128)S(1)} %copy.113, s32[]{:T(128)} %get-tuple-element.625, s32[]{:T(128)} %constant.189.clone.1..sunk.2, s32[]{:T(128)} %constant.189.clone.1..sunk.2) | dynamic-update-slice | bytes 524292 | tf_op jit(solution)/shard_map/while/body/eval_jaxpr/jit(dynamic_update_index_in_dim)/dynamic_update_slice | solution.py:168
  213.5 5.2 %scatter_fusion = f32[32,64,1024]{2,1,0:T(8,128)} fusion(f32[32,64,1024]{2,1,0:T(8,128)} %get-tuple-element.627, s32[8]{0:T(128)S(1)} %fusion.79, f32[8,64,1024]{2,1,0:T(8,128)} %bitcast.141), kind=kCustom, calls=%fused_computation.5.clone.clone.1 | custom fusion | flops 524288 | bytes 6291488 | tf_op jit(solution)/shard_map/while/body/eval_jaxpr/scatter-add | solution.py:172
  219.0 5.8 %dynamic_update_slice.51 = f32[4,64,1024]{2,0,1:T(4,128)} dynamic-update-slice(f32[4,64,1024]{2,0,1:T(4,128)} %get-tuple-element.628, f32[1,64,1024]{2,0,1:T(1,128)S(1)} %copy.113, s32[]{:T(128)} %get-tuple-element.625, s32[]{:T(128)} %constant.189.clone.1..sunk.2, s32[]{:T(128)} %constant.189.clone.1..sunk.2) | dynamic-update-slice | bytes 524292 | tf_op jit(solution)/shard_map/while/body/eval_jaxpr/jit(dynamic_update_index_in_dim)/dynamic_update_slice | solution.py:168
  231.6 5.1 %scatter_fusion = f32[32,64,1024]{2,1,0:T(8,128)} fusion(f32[32,64,1024]{2,1,0:T(8,128)} %get-tuple-element.627, s32[8]{0:T(128)S(1)} %fusion.79, f32[8,64,1024]{2,1,0:T(8,128)} %bitcast.141), kind=kCustom, calls=%fused_computation.5.clone.clone.1 | custom fusion | flops 524288 | bytes 6291488 | tf_op jit(solution)/shard_map/while/body/eval_jaxpr/scatter-add | solution.py:172
  237.1 5.8 %dynamic_update_slice.51 = f32[4,64,1024]{2,0,1:T(4,128)} dynamic-update-slice(f32[4,64,1024]{2,0,1:T(4,128)} %get-tuple-element.628, f32[1,64,1024]{2,0,1:T(1,128)S(1)} %copy.113, s32[]{:T(128)} %get-tuple-element.625, s32[]{:T(128)} %constant.189.clone.1..sunk.2, s32[]{:T(128)} %constant.189.clone.1..sunk.2) | dynamic-update-slice | bytes 524292 | tf_op jit(solution)/shard_map/while/body/eval_jaxpr/jit(dynamic_update_index_in_dim)/dynamic_update_slice | solution.py:168
  249.7 5.1 %scatter_fusion = f32[32,64,1024]{2,1,0:T(8,128)} fusion(f32[32,64,1024]{2,1,0:T(8,128)} %get-tuple-element.627, s32[8]{0:T(128)S(1)} %fusion.79, f32[8,64,1024]{2,1,0:T(8,128)} %bitcast.141), kind=kCustom, calls=%fused_computation.5.clone.clone.1 | custom fusion | flops 524288 | bytes 6291488 | tf_op jit(solution)/shard_map/while/body/eval_jaxpr/scatter-add | solution.py:172
  255.1 5.8 %dynamic_update_slice.51 = f32[4,64,1024]{2,0,1:T(4,128)} dynamic-update-slice(f32[4,64,1024]{2,0,1:T(4,128)} %get-tuple-element.628, f32[1,64,1024]{2,0,1:T(1,128)S(1)} %copy.113, s32[]{:T(128)} %get-tuple-element.625, s32[]{:T(128)} %constant.189.clone.1..sunk.2, s32[]{:T(128)} %constant.189.clone.1..sunk.2) | dynamic-update-slice | bytes 524292 | tf_op jit(solution)/shard_map/while/body/eval_jaxpr/jit(dynamic_update_index_in_dim)/dynamic_update_slice | solution.py:168
  261.0 28.3 %while.45 = (s32[]{:T(128)}, bf16[4,512,1024]{2,1,0:T(8,128)(2,1)}, bf16[4,576,512]{2,1,0:T(8,128)(2,1)}, s32[4]{0:T(128)S(1)}, bf16[4,64,1024]{2,1,0:T(8,128)(2...) while((s32[]{:T(128)}, bf16[4,512,1024]{2,1,0:T(8,128)(2,1)}, ...), condition=%wide.region_23.24_spmd, body=%wide.region_22.23_spmd.sunk | while | flops 604569600 | bytes 8586387 | solution.py:192
  272.0 3.1 bitcast_dynamic-update-slice_fusion.4
  289.3 4.0 convert_element_type.45
  293.3 6.3 %copy.88 = bf16[16,2,64,1024]{3,1,2,0:T(2,128)(2,1)} copy(bf16[16,2,64,1024]{3,2,1,0:T(8,128)(2,1)S(1)} %bitcast.146) | data formatting | bytes 8388608 | tf_op jit(solution)/shard_map/reshape | solution.py:199
  299.6 4.7 %all-to-all-start.4 = ((bf16[16,2,64,1024]{3,1,2,0:T(2,128)(2,1)}), bf16[16,2,64,1024]{3,1,2,0:T(2,128)(2,1)}, u32[]{:S(2)}, u32[]{:S(2)}) async-start(bf16[16,2,64,1024]{3,1,2,0:T(2,128)(2,1)} %copy.88), calls=%async_computation.5 | async-start | bytes 8388608 | tf_op jit(solution)/shard_map/all_to_all | solution.py:198
  305.6 111.3 %psum.15 = f32[]{:T(128)} all-reduce(f32[]{:T(128)S(6)} %add.200), channel_id=1, replica_groups=mesh['dp'=16,'inner'=8] {'dp','inner'}, use_global_device_ids=true, to_apply=%region_18.19 | all-reduce | flops 1 | bytes 8 | tf_op jit(solution)/shard_map/psum | solution.py:138
  417.5 4.8 %fusion.27 = bf16[4,64,1024]{2,0,1:T(4,128)(2,1)S(1)} fusion(f32[4,64,1024]{2,0,1:T(4,128)S(1)} %copy-done.3, bf16[16,2,64,1024]{3,1,2,0:T(2,128)(2,1)} %all-to-all-done.4, s32[16,2]{0,1:T(2,128)S(1)} %get-tuple-element.389, pred[16,2]{0,1:T(4,128)(4,1)S(1)} %get-tuple-element.385), kind=kOutput, calls=%fused_computation.52 | convolution fusion | flops 17301760 | bytes 5767328 | tf_op jit(solution)/shard_map/eg,ecd->gcd/dot_general | solution.py:205
  (217 shorter events, 78.7 us)
Async XLA Ops:
  7.2 76.7 %all-gather.2.cloned.1.call-start = ((), (), s32[]{:S(2)}) async-start(), calls=%async_computation.6 | async-start | bytes 8912896 | tf_op jit(solution)/shard_map/all_gather | solution.py:59
  11.4 7.0 %copy-start.4 = (s32[64,8]{0,1:T(8,128)S(1)}, s32[64,8]{0,1:T(8,128)}, u32[]{:S(2)}) copy-start(s32[64,8]{0,1:T(8,128)} %param.11) | copy-start | bytes 6148
  11.4 55.7 %all-to-all-start = ((bf16[8,4,64,1024]{3,2,1,0:T(8,128)(2,1)}), bf16[8,4,64,1024]{3,2,1,0:T(8,128)(2,1)}, u32[]{:S(2)}, u32[]{:S(2)}) async-start(bf16[8,4,64,1024]{3,2,1,0:T(8,128)(2,1)} %stack.2), calls=%async_computation | async-start | bytes 8388608 | tf_op jit(solution)/shard_map/all_to_all | solution.py:15
  18.4 3.6 copy-start.1
  18.4 3.6 copy-start.2
  123.9 33.7 %all-to-all-start.2 = ((f32[16,1,128]{2,1,0:T(1,128)}), f32[16,1,128]{2,1,0:T(1,128)S(1)}, u32[]{:S(2)}, u32[]{:S(2)}) async-start(f32[16,1,128]{2,1,0:T(1,128)} %reshape.344), calls=%async_computation.2 | async-start | bytes 16384 | tf_op jit(solution)/shard_map/all_to_all | solution.py:111
  157.6 12.7 %all-to-all-start.1 = ((f32[16,1,128]{2,1,0:T(1,128)}), f32[16,1,128]{2,1,0:T(1,128)S(1)}, u32[]{:S(2)}, u32[]{:S(2)}) async-start(f32[16,1,128]{2,1,0:T(1,128)} %reshape.342), calls=%async_computation.1 | async-start | bytes 16384 | tf_op jit(solution)/shard_map/all_to_all | solution.py:104
  173.3 9.8 %all-to-all-start.3 = ((f32[16,1,128]{2,1,0:T(1,128)}), f32[16,1,128]{2,1,0:T(1,128)S(1)}, u32[]{:S(2)}, u32[]{:S(2)}) async-start(f32[16,1,128]{2,1,0:T(1,128)} %reshape.346), calls=%async_computation.3 | async-start | bytes 16384 | tf_op jit(solution)/shard_map/all_to_all | solution.py:140
  176.7 246.5 %reduce-scatter.2.cloned.1.call-start = ((), (), s32[]{:S(2)}) async-start(), calls=%async_computation.7 | async-start | bytes 4718592 | tf_op jit(solution)/shard_map/reduce_scatter | solution.py:191
  188.8 2.5 copy-start
  206.8 2.5 copy-start
  224.8 2.5 copy-start
  242.9 2.5 copy-start
  299.6 117.9 %copy-start.3 = (f32[4,64,1024]{2,0,1:T(4,128)S(1)}, f32[4,64,1024]{2,0,1:T(4,128)}, u32[]{:S(2)}) copy-start(f32[4,64,1024]{2,0,1:T(4,128)} %get-tuple-element.278) | copy-start | bytes 3145732
  299.6 117.9 %all-to-all-start.4 = ((bf16[16,2,64,1024]{3,1,2,0:T(2,128)(2,1)}), bf16[16,2,64,1024]{3,1,2,0:T(2,128)(2,1)}, u32[]{:S(2)}, u32[]{:S(2)}) async-start(bf16[16,2,64,1024]{3,1,2,0:T(2,128)(2,1)} %copy.88), calls=%async_computation.5 | async-start | bytes 8388608 | tf_op jit(solution)/shard_map/all_to_all | solution.py:198
Sparse Core Ops, SparseCore 0:
  10.1 73.6 all-gather.1
  289.4 33.4 reduce-scatter.1
